TPU v7x, 256 devices: a whole 4x4x8 slice. The times are simulated.
256 devices in a mesh: row: 32 (over z, y_lo, core), col: 8 (over y_hi, x).
Axes of the slice: x: 4, y: 4 (y_hi: 2, y_lo: 2; y = y_hi * 2 + y_lo), z: 8, core: 2. Of those that a mesh axis runs over, the one named last changes fastest.
Arguments:
- features: bfloat16 [32768, 128], P(('col', 'row')), may hold values from -96 to 96
- weight: bfloat16 [128, 256], replicated, may hold values from -0.5 to 0.5
- bias: float32 [256], replicated, may hold values from -3 to 3
- cotangent: bfloat16 [32768, 256], P(('row', 'col')), may hold values from -6 to 6
- tile_values: bfloat16 [32, 8, 256, 128, 128], P('row', 'col'), may hold values from 0 to 4, as said below
- tile_pos: int32 [32, 8, 2, 256], P('row', 'col'), may hold values from 0 to 31, as said below
- tile_count: int32 [32, 8], P('row', 'col'), may hold values from 0 to 256, as said below
- block_perm: int32 [256], replicated, may hold values from 0 to 255, as said below
Outputs:
- hidden: bfloat16 [32768, 256], P(('row', 'col'))
- weight_grad: float32 [128, 256], replicated
- bias_grad: float32 [256], replicated
Inputs may be any that keep to these rules, and one draw needn't show every extreme that they name: `tile_values`: entries are 0 or a weight of at least 0.25; slots t at or beyond tile_count[r, c] belong to no tile. `tile_pos`: entry [r, c, 0, t] is the slot's tile row, below 8, within row block r, and [r, c, 1, t] its tile column, below 32, within column block c, both in the reordered numbering; the slots of one cell hold distinct positions. `tile_count`: every draw has a cell with 256 live slots. `block_perm`: each aligned run of 8 entries is a permutation of that run's own indices.
All inputs are finite; a program needn't handle non-finite values.
Results may differ from a plain program's by a relative error of at most 0.0059.
Values may be sent and summed in bfloat16 or wider, within the bound.
No kernel may reach another device: no remote copies, remote signals or barrier semaphores. Data moves between devices by JAX's collectives and lax.ppermute only.
A program may use at most 64 MiB of HBM per device.

v0:
```python
import jax
import jax.numpy as jnp
from jax import lax
from jax.sharding import PartitionSpec as P


def local_index(block_perm, tile_axis, block_index, run_length):
    return jnp.take(block_perm, block_index * run_length + tile_axis) - block_index * run_length


def body(features, weight, bias, cotangent, tile_values, tile_pos, tile_count, block_perm):
    row_count = lax.axis_size("row")
    col_count = lax.axis_size("col")
    row_index = lax.axis_index("row")
    col_index = lax.axis_index("col")
    packed = tile_values[0, 0]
    positions = tile_pos[0, 0]
    live_count = tile_count[0, 0]
    max_tiles = packed.shape[0]
    tile_size = packed.shape[1]
    feat_width = features.shape[1]
    row_tiles = block_perm.shape[0] // row_count
    col_tiles = row_tiles * row_count // col_count
    block_tiles = min(64, max_tiles)
    lane_index = jnp.arange(block_tiles, dtype=jnp.int32)
    own_rows = local_index(block_perm, positions[0], row_index, row_tiles)
    own_cols = local_index(block_perm, positions[1], col_index, col_tiles)

    def degree_step(block_step, totals):
        row_acc, col_acc = totals
        slot_number = block_step * block_tiles + lane_index
        is_live = slot_number < live_count
        clamped = jnp.minimum(slot_number, max_tiles - 1)
        values = jnp.take(packed, clamped, axis=0).astype(jnp.float32)
        row_part = jnp.sum(values, axis=2)
        col_part = jnp.sum(values, axis=1)
        row_part = jnp.where(is_live[:, None], row_part, 0.0)
        col_part = jnp.where(is_live[:, None], col_part, 0.0)
        row_acc = row_acc.at[jnp.take(own_rows, clamped)].add(row_part)
        col_acc = col_acc.at[jnp.take(own_cols, clamped)].add(col_part)
        return (row_acc, col_acc)

    degree_blocks = (live_count + block_tiles - 1) // block_tiles
    row_acc, col_acc = lax.fori_loop(
        jnp.int32(0),
        degree_blocks,
        degree_step,
        (
            jnp.zeros((row_tiles, tile_size), jnp.float32),
            jnp.zeros((col_tiles, tile_size), jnp.float32),
        ),
    )
    col_part_flat = col_acc.reshape(col_tiles * tile_size)
    col_share = lax.psum_scatter(col_part_flat, "row", scatter_dimension=0, tiled=True)
    scaled = (lax.rsqrt(1.0 + col_share)[:, None] * features.astype(jnp.float32)).astype(
        jnp.bfloat16
    )
    gathered = lax.all_gather(scaled, "row", axis=0, tiled=True)
    feature_tiles = gathered.reshape(col_tiles, tile_size, feat_width)
    list_length = packed.shape[0]

    def product_step(block_step, partial_value):
        logical = block_step * block_tiles + lane_index
        is_live = logical < live_count
        is_upper = logical >= live_count
        source = jnp.where(is_upper, logical - live_count, logical)
        source = jnp.clip(source, 0, list_length - 1)
        slot_number = jnp.minimum(is_upper.astype(jnp.int32), 1 - 1)
        tile_block = jnp.take(packed, source, axis=0)
        tile_block = jnp.where(is_live[:, None, None], tile_block, jnp.zeros((), jnp.bfloat16))
        inputs = jnp.take(feature_tiles, jnp.take(own_cols, source), axis=0)
        products = jnp.einsum(
            "bpq,bqf->bpf", tile_block, inputs, preferred_element_type=jnp.float32
        )
        return partial_value.at[slot_number, jnp.take(own_rows, source)].add(products)

    product_blocks = (live_count + block_tiles - 1) // block_tiles
    initial = jnp.zeros((1, row_tiles, tile_size, feat_width), jnp.float32)
    partial_value = lax.fori_loop(jnp.int32(0), product_blocks, product_step, initial)
    own_sum = partial_value[0]
    row_part_flat = row_acc.reshape(row_tiles * tile_size)
    summed, degree_share = (
        lax.psum_scatter(
            own_sum.reshape(row_tiles * tile_size, feat_width),
            "col",
            scatter_dimension=0,
            tiled=True,
        ),
        lax.psum_scatter(row_part_flat, "col", scatter_dimension=0, tiled=True),
    )
    aggregated = (lax.rsqrt(1.0 + degree_share)[:, None] * summed).astype(jnp.bfloat16)
    preact = jnp.dot(aggregated, weight, preferred_element_type=jnp.float32) + bias
    logistic = jax.nn.sigmoid(preact)
    hidden = (preact * logistic).astype(jnp.bfloat16)
    preact_grad = (
        cotangent.astype(jnp.float32) * logistic * (1.0 + preact * (1.0 - logistic))
    ).astype(jnp.bfloat16)
    weight_part = jnp.einsum(
        "nf,nh->fh", aggregated, preact_grad, preferred_element_type=jnp.float32
    )
    bias_part = jnp.sum(preact_grad.astype(jnp.float32), axis=0)
    weight_sum, bias_sum = lax.psum((weight_part, bias_part), ("row", "col"))
    inverse_root = lax.rsqrt(jnp.float32(summed.shape[0] * row_count * col_count))
    return (hidden, weight_sum * inverse_root, bias_sum * inverse_root)


def solution(mesh):
    placed = (
        P(("col", "row"), None),
        P(),
        P(),
        P(("row", "col"), None),
        P("row", "col", None, None, None),
        P("row", "col", None, None),
        P("row", "col"),
        P(),
    )
    return jax.shard_map(
        body,
        mesh=mesh,
        in_specs=placed,
        out_specs=(P(("row", "col"), None), P(), P()),
        check_vma=False,
    )
```

profile of v0, /device:TPU:2, one launch (start us, length us, event | category | flops | bytes accessed | tf_op | source)
XLA Modules:
  0.0 723.7 jit_solution(14614431443404107920)
XLA Ops:
  7.2 0.0 copy-start
  7.2 0.0 all-gather.2.cloned.1.call-start
  7.9 0.8 slice_add_fusion
  8.7 2.0 gather_fusion.8
  10.7 2.0 gather_fusion.7
  12.7 0.0 copy-start.8
  12.7 0.0 copy-start.4
  12.7 0.0 copy-start.5
  12.7 9.5 %while.24 = (s32[]{:T(128)}, f32[8,128]{1,0:T(8,128)S(1)}, f32[32,128]{1,0:T(8,128)S(1)}, s32[]{:T(128)}, s32[256]{0:T(256)S(1)}, /*index=5*/s32[]{:T(128)}, bf1...) while((s32[]{:T(128)}, f32[8,128]{1,0:T(8,128)S(1)}, ...), condition=%wide.region_5.9_spmd.clone, body=%wide.region_0.8_spmd.clone.sunk | while | flops 4213635 | bytes 6451793 | solution.py:44
  12.8 0.7 compare_and_fusion.6
  13.4 0.8 gather_fusion.1
  14.2 0.8 gather_fusion
  15.0 4.3 gather_fusion.2
  19.4 0.9 convert_reduce_fusion.4
  20.2 1.0 scatter_custom_fusion.15
  21.2 1.0 scatter_custom_fusion.16
  22.2 122.7 %all-reduce.1 = f32[4096]{0:T(1024)S(1)} all-reduce(f32[4096]{0:T(1024)S(1)} %bitcast.44), channel_id=3, replica_groups=mesh['row'=32,'col'=8] {'row'}, use_global_device_ids=true, to_apply=%region_7.11.clone | all-reduce | flops 4096 | bytes 32768
  145.0 0.6 dynamic-slice.2
  146.2 0.1 fusion.31
  146.3 0.7 multiply_convert_fusion.3
  147.0 0.0 all-gather.2.cloned.1.call-update
  147.0 0.0 reduce-scatter.2.cloned.1.call-start
  147.1 74.5 %all-gather.2.cloned.1.call-done = bf16[4096,128]{1,0:T(8,128)(2,1)} async-done(((bf16[128,128]{1,0:T(8,128)(2,1)}), bf16[4096,128]{1,0:T(8,128)(2,1)}) %all-gather.2.cloned.1.call-update) | async-done | bytes 1048592 | tf_op jit(solution)/shard_map/all_gather | solution.py:58
  221.6 0.0 copy-start.7
  221.6 0.0 copy-start.6
  221.6 24.0 %while.25 = (s32[]{:T(128)}, f32[1,8,128,128]{3,2,1,0:T(8,128)S(1)}, s32[]{:T(128)}, s32[]{:T(128)}, s32[256]{0:T(256)S(1)}, /*index=5*/bf16[256,128,128]{2,1,0:...) while((s32[]{:T(128)}, f32[1,8,128,128]{3,2,1,0:T(8,128)S(1)}, ...), condition=%wide.region_10.14_spmd.clone, body=%wide.region_8.13_spmd.clone.sunk | while | flops 272634240 | bytes 41956408 | solution.py:79
  221.6 0.7 compare_and_fusion.7
  222.4 0.8 gather_fusion.5
  223.2 0.8 gather_fusion.3
  224.0 0.7 fusion.44
  224.7 2.2 gather_fusion.6
  226.8 5.7 gather_fusion.4
  232.5 4.3 fusion.45
  236.8 8.8 %scatter_fusion = f32[8,128,128]{2,1,0:T(8,128)S(1)} fusion(f32[8,128,128]{2,1,0:T(8,128)S(1)} %bitcast.39, s32[64]{0:T(128)S(1)} %fusion.44, f32[64,128,128]{2,1,0:T(8,128)} %fusion.45), kind=kCustom, calls=%fused_computation.11.clone.clone.1 | custom fusion | flops 1048576 | bytes 12583168 | tf_op jit(solution)/shard_map/while/body/scatter-add | solution.py:75
  245.6 0.8 copy-done.1
  246.4 0.0 reduce-scatter.2.cloned.1.call-update
  246.4 0.0 all-reduce.4.cloned.1.call-start
  246.5 0.6 dynamic-slice
  247.7 43.6 %all-reduce = f32[1024]{0:T(1024)S(1)} all-reduce(f32[1024]{0:T(1024)S(1)} %bitcast.45), channel_id=2, replica_groups=mesh['row'=32,'col'=8] {'col'}, use_global_device_ids=true, to_apply=%region_6.10.clone | all-reduce | flops 1024 | bytes 8192
  291.3 0.1 fusion.32
  291.4 102.7 %reduce-scatter.2.cloned.1.call-done = f32[128,128]{1,0:T(8,128)} async-done(((f32[1024,128]{1,0:T(8,128)}), f32[128,128]{1,0:T(8,128)}) %reduce-scatter.2.cloned.1.call-update) | async-done | bytes 65552 | tf_op jit(solution)/shard_map/reduce_scatter | solution.py:83
  394.1 1.7 convert_reduce_fusion.2
  395.8 73.9 %psum.15 = f32[256]{0:T(256)S(1)} all-reduce(f32[256]{0:T(256)S(1)} %get-tuple-element.182), channel_id=1, replica_groups=mesh['row'=32,'col'=8] {'row','col'}, use_global_device_ids=true, to_apply=%region_14.18 | all-reduce | flops 256 | bytes 2048 | tf_op jit(solution)/shard_map/psum | solution.py:102
  469.8 1.8 fusion.33
  471.6 0.0 all-reduce.4.cloned.1.call-update
  471.6 0.6 broadcast_multiply_fusion.1
  472.1 243.5 %all-reduce.4.cloned.1.call-done = f32[128,256]{1,0:T(8,128)} async-done(((f32[128,256]{1,0:T(8,128)}), f32[128,256]{1,0:T(8,128)}) %all-reduce.4.cloned.1.call-update) | async-done | bytes 131088 | tf_op jit(solution)/shard_map/psum | solution.py:102
  715.6 1.6 broadcast_multiply_fusion
  (25 shorter events, 0.1 us)
Async XLA Ops:
  7.2 386.9 %copy-start = (bf16[128,256]{1,0:T(8,128)(2,1)S(1)}, bf16[128,256]{1,0:T(8,128)(2,1)}, u32[]{:S(2)}) copy-start(bf16[128,256]{1,0:T(8,128)(2,1)} %param.19) | copy-start | bytes 196612
  7.2 214.3 %all-gather.2.cloned.1.call-start = ((), (), s32[]{:S(2)}) async-start(), calls=%async_computation.1 | async-start | bytes 1081344 | tf_op jit(solution)/shard_map/all_gather | solution.py:58
  12.7 132.3 %copy-start.8 = (u32[256]{0:T(256)S(1)}, u32[256]{0:T(256)}, u32[]{:S(2)}) copy-start(u32[256]{0:T(256)} %constant.133) | copy-start | bytes 3076
  12.7 133.6 %copy-start.4 = (bf16[128,128]{1,0:T(8,128)(2,1)S(1)}, bf16[128,128]{1,0:T(8,128)(2,1)}, u32[]{:S(2)}) copy-start(bf16[128,128]{1,0:T(8,128)(2,1)} %param.18) | copy-start | bytes 98308
  12.7 381.4 %copy-start.5 = (bf16[128,256]{1,0:T(8,128)(2,1)S(1)}, bf16[128,256]{1,0:T(8,128)(2,1)}, u32[]{:S(2)}) copy-start(bf16[128,256]{1,0:T(8,128)(2,1)} %param.21) | copy-start | bytes 196612
  147.0 247.1 %reduce-scatter.2.cloned.1.call-start = ((), (), s32[]{:S(2)}) async-start(), calls=%async_computation.2 | async-start | bytes 589824 | tf_op jit(solution)/shard_map/reduce_scatter | solution.py:83
  221.6 24.9 %copy-start.7 = (u32[256]{0:T(256)S(1)}, u32[256]{0:T(256)}, u32[]{:S(2)}) copy-start(u32[256]{0:T(256)} %constant.129) | copy-start | bytes 3076
  221.6 172.5 %copy-start.6 = (f32[256]{0:T(256)S(1)}, f32[256]{0:T(256)}, u32[]{:S(2)}) copy-start(f32[256]{0:T(256)} %param.20) | copy-start | bytes 3076
  221.6 3.1 copy-start.2
  226.8 5.7 copy-start.3
  245.6 0.8 copy-start.1
  246.4 469.2 %all-reduce.4.cloned.1.call-start = ((), (), s32[]{:S(2)}) async-start(), calls=%async_computation.3 | async-start | bytes 262144 | tf_op jit(solution)/shard_map/psum | solution.py:102
Sparse Core Ops, SparseCore 0:
  147.1 74.3 all-gather.1
  246.6 147.4 reduce-scatter.1
  471.7 243.8 all-reduce.3
where the time goes:
time: 725 us; the launch traced here: 724 us
  waiting for transfers between devices  421 us (58%)
  blocking collectives  240 us (33%)
  local copies, waits for them, and re-layouts  21.3 us (3%)
  other arithmetic  17.5 us (2%)
  between operations  15.9 us (2%)
  matrix products  7.81 us (1%)
    psum x1, waiting for transfers between devices, body(): weight_sum, bias_sum = lax.psum((weight_part, bias_part), ('row', 'col'))  243 us
    unnamed x2, blocking collectives  166 us
    reduce_scatter x1, waiting for transfers between devices, body(): lax.psum_scatter(own_sum.reshape(row_tiles * tile_size, feat_width), 'col...  103 us
    all_gather x1, waiting for transfers between devices, body(): gathered = lax.all_gather(scaled, 'row', axis=0, tiled=True)  74.5 us
    psum x1, blocking collectives, body(): weight_sum, bias_sum = lax.psum((weight_part, bias_part), ('row', 'col'))  73.9 us
  transfers between devices with their start and end apart: 3, of which 3 were waited for; matrix products, arithmetic and copies ran while one was open for 0% of the time, Pallas kernels for 0%

commit v1 on v0

--- a/solution.py
+++ b/solution.py
@@ -99,7 +99,7 @@
         "nf,nh->fh", aggregated, preact_grad, preferred_element_type=jnp.float32
     )
     bias_part = jnp.sum(preact_grad.astype(jnp.float32), axis=0)
-    weight_sum, bias_sum = lax.psum((weight_part, bias_part), ("row", "col"))
+    weight_sum, bias_sum = lax.psum(lax.psum((weight_part, bias_part), "col"), "row")
     inverse_root = lax.rsqrt(jnp.float32(summed.shape[0] * row_count * col_count))
     return (hidden, weight_sum * inverse_root, bias_sum * inverse_root)
 

time: 725 us -> 702 us (0.968)
  waiting for transfers between devices: 421 us -> 399 us
    psum x1 -> x2, waiting for transfers between devices: 243 us -> 222 us  [the longest x1 209 us: body(): lax.psum(lax.psum((weight_part, bias_part), 'col'), 'row')]
    psum x1 -> x2, blocking collectives: 73.9 us -> 72.8 us  [the longest x1 53 us: body(): lax.psum(lax.psum((weight_part, bias_part), 'col'), 'row')]
  transfers between devices with their start and end apart: 3 -> 4, of which waited for: 3 -> 4; matrix products, arithmetic and copies ran while one was open for 0% -> 0% of each run, Pallas kernels for 0% -> 0%
where the time goes in v1:
time: 702 us; the launch traced here: 701 us
  waiting for transfers between devices  399 us (57%)
  blocking collectives  239 us (34%)
  local copies, waits for them, and re-layouts  21.3 us (3%)
  other arithmetic  17.5 us (2%)
  between operations  15.9 us (2%)
  matrix products  7.81 us (1%)
    psum x1, waiting for transfers between devices, body(): lax.psum(lax.psum((weight_part, bias_part), 'col'), 'row')  209 us
    unnamed x2, blocking collectives  166 us
    reduce_scatter x1, waiting for transfers between devices, body(): lax.psum_scatter(own_sum.reshape(row_tiles * tile_size, feat_width), 'col...  103 us
    all_gather x1, waiting for transfers between devices, body(): gathered = lax.all_gather(scaled, 'row', axis=0, tiled=True)  74.5 us
    psum x1, blocking collectives, body(): lax.psum(lax.psum((weight_part, bias_part), 'col'), 'row')  53 us
    psum x1, blocking collectives, body(): lax.psum((weight_part, bias_part), 'col')  19.8 us
  transfers between devices with their start and end apart: 4, of which 4 were waited for; matrix products, arithmetic and copies ran while one was open for 0% of the time, Pallas kernels for 0%

profile of v1, /device:TPU:2, one launch (start us, length us, event | category | flops | bytes accessed | tf_op | source)
XLA Modules:
  0.0 700.8 jit_solution(10879429908123594634)
XLA Ops:
  7.2 0.0 copy-start
  7.2 0.0 all-gather.2.cloned.1.call-start
  7.9 0.8 slice_add_fusion
  8.7 2.0 gather_fusion.8
  10.7 2.0 gather_fusion.7
  12.7 0.0 copy-start.8
  12.7 9.5 %while.24 = (s32[]{:T(128)}, f32[8,128]{1,0:T(8,128)S(1)}, f32[32,128]{1,0:T(8,128)S(1)}, s32[]{:T(128)}, s32[256]{0:T(256)S(1)}, /*index=5*/s32[]{:T(128)}, bf1...) while((s32[]{:T(128)}, f32[8,128]{1,0:T(8,128)S(1)}, ...), condition=%wide.region_5.9_spmd.clone, body=%wide.region_0.8_spmd.clone.sunk | while | flops 4213635 | bytes 6451793 | solution.py:44
  12.8 0.7 compare_and_fusion.6
  13.4 0.8 gather_fusion.1
  14.2 0.8 gather_fusion
  15.0 4.3 gather_fusion.2
  19.4 0.9 convert_reduce_fusion.4
  20.2 1.0 scatter_custom_fusion.15
  21.2 1.0 scatter_custom_fusion.16
  22.2 122.7 %all-reduce.1 = f32[4096]{0:T(1024)S(1)} all-reduce(f32[4096]{0:T(1024)S(1)} %bitcast.44), channel_id=3, replica_groups=mesh['row'=32,'col'=8] {'row'}, use_global_device_ids=true, to_apply=%region_7.11.clone | all-reduce | flops 4096 | bytes 32768
  145.0 0.6 dynamic-slice.2
  146.2 0.1 fusion.31
  146.3 0.7 multiply_convert_fusion.3
  147.0 0.0 all-gather.2.cloned.1.call-update
  147.0 0.0 reduce-scatter.2.cloned.1.call-start
  147.1 74.5 %all-gather.2.cloned.1.call-done = bf16[4096,128]{1,0:T(8,128)(2,1)} async-done(((bf16[128,128]{1,0:T(8,128)(2,1)}), bf16[4096,128]{1,0:T(8,128)(2,1)}) %all-gather.2.cloned.1.call-update) | async-done | bytes 1048592 | tf_op jit(solution)/shard_map/all_gather | solution.py:58
  221.6 24.0 %while.25 = (s32[]{:T(128)}, f32[1,8,128,128]{3,2,1,0:T(8,128)S(1)}, s32[]{:T(128)}, s32[]{:T(128)}, s32[256]{0:T(256)S(1)}, /*index=5*/bf16[256,128,128]{2,1,0:...) while((s32[]{:T(128)}, f32[1,8,128,128]{3,2,1,0:T(8,128)S(1)}, ...), condition=%wide.region_10.14_spmd.clone, body=%wide.region_8.13_spmd.clone.sunk | while | flops 272634240 | bytes 41956408 | solution.py:79
  221.6 0.7 compare_and_fusion.7
  222.4 0.8 gather_fusion.5
  223.2 0.8 gather_fusion.3
  224.0 0.7 fusion.44
  224.7 2.2 gather_fusion.6
  226.8 5.7 gather_fusion.4
  232.5 4.3 fusion.45
  236.8 8.8 %scatter_fusion = f32[8,128,128]{2,1,0:T(8,128)S(1)} fusion(f32[8,128,128]{2,1,0:T(8,128)S(1)} %bitcast.39, s32[64]{0:T(128)S(1)} %fusion.44, f32[64,128,128]{2,1,0:T(8,128)} %fusion.45), kind=kCustom, calls=%fused_computation.11.clone.clone.1 | custom fusion | flops 1048576 | bytes 12583168 | tf_op jit(solution)/shard_map/while/body/scatter-add | solution.py:75
  245.6 0.8 copy-done.1
  246.4 0.0 reduce-scatter.2.cloned.1.call-update
  246.4 0.0 all-reduce.5.cloned.1.call-start
  246.5 0.6 dynamic-slice
  247.7 43.6 %all-reduce = f32[1024]{0:T(1024)S(1)} all-reduce(f32[1024]{0:T(1024)S(1)} %bitcast.45), channel_id=2, replica_groups=mesh['row'=32,'col'=8] {'col'}, use_global_device_ids=true, to_apply=%region_6.10.clone | all-reduce | flops 1024 | bytes 8192
  291.3 0.1 fusion.32
  291.4 102.7 %reduce-scatter.2.cloned.1.call-done = f32[128,128]{1,0:T(8,128)} async-done(((f32[1024,128]{1,0:T(8,128)}), f32[128,128]{1,0:T(8,128)}) %reduce-scatter.2.cloned.1.call-update) | async-done | bytes 65552 | tf_op jit(solution)/shard_map/reduce_scatter | solution.py:83
  394.1 1.7 convert_reduce_fusion.2
  395.8 1.8 fusion.33
  397.6 0.0 all-reduce.5.cloned.1.call-update
  397.6 0.0 all-reduce.7.cloned.1.call-start
  397.7 19.8 %psum.30 = f32[256]{0:T(256)S(1)} all-reduce(f32[256]{0:T(256)S(1)} %get-tuple-element.182), channel_id=1, replica_groups=mesh['row'=32,'col'=8] {'col'}, use_global_device_ids=true, to_apply=%region_15.19 | all-reduce | flops 256 | bytes 2048 | tf_op jit(solution)/shard_map/psum | solution.py:102
  417.5 53.0 %psum.31 = f32[256]{0:T(256)S(1)} all-reduce(f32[256]{0:T(256)S(1)} %psum.30), channel_id=1, replica_groups=mesh['row'=32,'col'=8] {'row'}, use_global_device_ids=true, to_apply=%region_16.20 | all-reduce | flops 256 | bytes 2048 | tf_op jit(solution)/shard_map/psum | solution.py:102
  470.4 12.8 %all-reduce.5.cloned.1.call-done = f32[128,256]{1,0:T(8,128)} async-done(((f32[128,256]{1,0:T(8,128)}), f32[128,256]{1,0:T(8,128)}) %all-reduce.5.cloned.1.call-update) | async-done | bytes 131088 | tf_op jit(solution)/shard_map/psum | solution.py:102
  483.2 0.0 all-reduce.7.cloned.1.call-update
  483.3 0.6 broadcast_multiply_fusion.1
  483.8 208.9 %all-reduce.7.cloned.1.call-done = f32[128,256]{1,0:T(8,128)} async-done(((f32[128,256]{1,0:T(8,128)}), f32[128,256]{1,0:T(8,128)}) %all-reduce.7.cloned.1.call-update) | async-done | bytes 131088 | tf_op jit(solution)/shard_map/psum | solution.py:102
  692.7 1.6 broadcast_multiply_fusion
  (29 shorter events, 0.2 us)
Async XLA Ops:
  7.2 386.9 %copy-start = (bf16[128,256]{1,0:T(8,128)(2,1)S(1)}, bf16[128,256]{1,0:T(8,128)(2,1)}, u32[]{:S(2)}) copy-start(bf16[128,256]{1,0:T(8,128)(2,1)} %param.19) | copy-start | bytes 196612
  7.2 214.3 %all-gather.2.cloned.1.call-start = ((), (), s32[]{:S(2)}) async-start(), calls=%async_computation.1 | async-start | bytes 1081344 | tf_op jit(solution)/shard_map/all_gather | solution.py:58
  12.7 132.3 %copy-start.8 = (u32[256]{0:T(256)S(1)}, u32[256]{0:T(256)}, u32[]{:S(2)}) copy-start(u32[256]{0:T(256)} %constant.133) | copy-start | bytes 3076
  12.7 133.6 %copy-start.4 = (bf16[128,128]{1,0:T(8,128)(2,1)S(1)}, bf16[128,128]{1,0:T(8,128)(2,1)}, u32[]{:S(2)}) copy-start(bf16[128,128]{1,0:T(8,128)(2,1)} %param.18) | copy-start | bytes 98308
  12.7 381.4 %copy-start.5 = (bf16[128,256]{1,0:T(8,128)(2,1)S(1)}, bf16[128,256]{1,0:T(8,128)(2,1)}, u32[]{:S(2)}) copy-start(bf16[128,256]{1,0:T(8,128)(2,1)} %param.21) | copy-start | bytes 196612
  147.0 247.1 %reduce-scatter.2.cloned.1.call-start = ((), (), s32[]{:S(2)}) async-start(), calls=%async_computation.2 | async-start | bytes 589824 | tf_op jit(solution)/shard_map/reduce_scatter | solution.py:83
  221.6 24.9 %copy-start.7 = (u32[256]{0:T(256)S(1)}, u32[256]{0:T(256)}, u32[]{:S(2)}) copy-start(u32[256]{0:T(256)} %constant.129) | copy-start | bytes 3076
  221.6 172.5 %copy-start.6 = (f32[256]{0:T(256)S(1)}, f32[256]{0:T(256)}, u32[]{:S(2)}) copy-start(f32[256]{0:T(256)} %param.20) | copy-start | bytes 3076
  221.6 3.1 copy-start.2
  226.8 5.7 copy-start.3
  245.6 0.8 copy-start.1
  246.4 236.8 %all-reduce.5.cloned.1.call-start = ((), (), s32[]{:S(2)}) async-start(), calls=%async_computation.3 | async-start | bytes 262144 | tf_op jit(solution)/shard_map/psum | solution.py:102
  397.6 295.1 %all-reduce.7.cloned.1.call-start = ((), (), s32[]{:S(2)}) async-start(), calls=%async_computation.4 | async-start | bytes 262144 | tf_op jit(solution)/shard_map/psum | solution.py:102
Sparse Core Ops, SparseCore 0:
  147.1 74.3 all-gather.1
  246.6 147.4 reduce-scatter.1
  397.7 85.4 all-reduce.4
  485.7 206.9 all-reduce.6
